TPU v7x, 128 devices: a whole 4x4x4 slice. The times are simulated.
128 devices in a mesh: ent: 32 (over x_hi, z, y), sec: 4 (over x_lo, core).
Axes of the slice: x: 4 (x_hi: 2, x_lo: 2; x = x_hi * 2 + x_lo), y: 4, z: 4, core: 2. Of those that a mesh axis runs over, the one named last changes fastest.
Arguments:
- features: bfloat16 [4096, 256], P('ent'), may hold values from -6 to 6
- theta: bfloat16 [256, 256], replicated, may hold values from -3 to 3
- section_weight: float32 [65536], P(('ent', 'sec')), may hold values from 0.5 to 2
- pair_rows: int32 [128, 32, 512], P(('ent', 'sec')), may hold values from 0 to 511
- pair_cols: int32 [128, 32, 512], P(('ent', 'sec')), may hold values from 0 to 127
- pair_counts: int32 [128, 32], P(('ent', 'sec')), may hold values from 0 to 512, as said below
- cotangent: bfloat16 [4096, 256], P('ent'), may hold values from -24 to 24
Outputs:
- activated: bfloat16 [4096, 256], P('ent')
- grad_features: bfloat16 [4096, 256], P('ent')
- grad_theta: float32 [256, 256], replicated
- grad_weight: float32 [65536], P(('ent', 'sec'))
Inputs may be any that keep to these rules, and one draw needn't show every extreme that they name: Only the first pair_counts[k, j] slots of shard k and block j are used; some shard uses all 512 slots of some block.
All inputs are finite; a program needn't handle non-finite values.
Results may differ from a plain program's by a relative error of at most 0.0059.
Values may be sent and summed in bfloat16 or wider, within the bound.
A program may use at most 64 MiB of HBM per device.

v0:
```python
import jax
import jax.numpy as jnp
from jax import lax
from jax.sharding import PartitionSpec as P


def hot_table(indices, live_slots, offset, table_width):
    hits = (indices - offset)[:, None] == jnp.arange(table_width, dtype=jnp.int32)[None, :]
    return (hits & live_slots[:, None]).astype(jnp.bfloat16)


def body(features, theta, section_weight, pair_rows, pair_cols, pair_counts, cotangent):
    ent_dev = features.shape[0]
    feature_width = features.shape[1]
    sec_dev = section_weight.shape[0]
    blocks_count = pair_rows.shape[1]
    slot_count = pair_rows.shape[2]
    own_block = lax.axis_index("ent")
    row_lists = pair_rows[0]
    col_lists = pair_cols[0]
    usable = jnp.arange(slot_count, dtype=jnp.int32)[None, :] < pair_counts[0][:, None]
    usable_float = usable.astype(jnp.float32)
    entity_index = jnp.arange(blocks_count, dtype=jnp.int32)[:, None] * ent_dev + col_lists
    local_degree = jax.ops.segment_sum(
        usable_float.reshape(-1), entity_index.reshape(-1), num_segments=blocks_count * ent_dev
    )
    entity_degree = lax.psum(local_degree, ("ent", "sec"))
    own_degree = lax.dynamic_slice_in_dim(entity_degree, own_block * ent_dev, ent_dev)
    entity_scale = lax.rsqrt(1.0 + own_degree)[:, None]
    sec_count = jax.ops.segment_sum(
        usable_float.reshape(-1), row_lists.reshape(-1), num_segments=sec_dev
    )
    section_scale = (section_weight / (1.0 + sec_count))[:, None]

    def entity_fold(running, incoming, start_row):
        row_count = incoming.shape[0]
        span_width = min(row_count, ent_dev)
        block_span = max(row_count // ent_dev, 1)
        offset = start_row

        def add_block(turn_index, accum):
            row_slots = lax.dynamic_index_in_dim(row_lists, turn_index, 0, keepdims=False)
            col_slots = lax.dynamic_index_in_dim(col_lists, turn_index, 0, keepdims=False)
            live_slots = lax.dynamic_index_in_dim(usable, turn_index, 0, keepdims=False)
            values = lax.dynamic_slice_in_dim(incoming, turn_index * span_width, span_width, 0)
            col_hot = hot_table(col_slots, live_slots, offset, span_width)
            row_hot = hot_table(row_slots, live_slots, 0, sec_dev)
            picked = jnp.dot(col_hot, values, preferred_element_type=jnp.float32).astype(
                jnp.bfloat16
            )
            return accum + jnp.einsum(
                "ps,pf->sf", row_hot, picked, preferred_element_type=jnp.float32
            )

        return lax.fori_loop(0, block_span, add_block, running)

    def entity_terms(messages, start_row):
        span_width = min(lax.axis_size("ent") * ent_dev, ent_dev)
        block_span = max(lax.axis_size("ent") * ent_dev // ent_dev, 1)
        offset = start_row

        def block_term(turn_index):
            row_slots = lax.dynamic_index_in_dim(row_lists, turn_index, 0, keepdims=False)
            col_slots = lax.dynamic_index_in_dim(col_lists, turn_index, 0, keepdims=False)
            live_slots = lax.dynamic_index_in_dim(usable, turn_index, 0, keepdims=False)
            row_hot = hot_table(row_slots, live_slots, 0, sec_dev)
            col_hot = hot_table(col_slots, live_slots, offset, span_width)
            picked = jnp.dot(row_hot, messages, preferred_element_type=jnp.float32).astype(
                jnp.bfloat16
            )
            return jnp.einsum("pw,pf->wf", col_hot, picked, preferred_element_type=jnp.float32)

        pieces = lax.map(block_term, jnp.arange(block_span, dtype=jnp.int32))
        return pieces.reshape(block_span * span_width, feature_width)

    def collect(messages):
        partial_sum = lax.psum_scatter(
            entity_terms(messages, jnp.int32(0)), "ent", scatter_dimension=0, tiled=True
        )
        return lax.psum(partial_sum, "sec")

    zero_sections = jnp.zeros((sec_dev, feature_width), jnp.float32)
    projected = jnp.dot(features, theta, preferred_element_type=jnp.float32)
    scaled = (entity_scale * projected).astype(jnp.bfloat16)
    gathered = entity_fold(
        zero_sections, lax.all_gather(scaled, "ent", axis=0, tiled=True), jnp.int32(0)
    )
    messages = (section_scale * gathered).astype(jnp.bfloat16)
    collected = collect(messages)
    preact = entity_scale * collected
    activated = jax.nn.silu(preact).astype(jnp.bfloat16)
    sigmoid_pre = jax.nn.sigmoid(preact)
    grad_pre = cotangent.astype(jnp.float32) * sigmoid_pre * (1.0 + preact * (1.0 - sigmoid_pre))
    back_scaled = (entity_scale * grad_pre).astype(jnp.bfloat16)
    back_gathered = entity_fold(
        zero_sections, lax.all_gather(back_scaled, "ent", axis=0, tiled=True), jnp.int32(0)
    )
    grad_weight = jnp.sum(gathered * back_gathered, axis=1) / (1.0 + sec_count)
    back_messages = (section_scale * back_gathered).astype(jnp.bfloat16)
    back_collected = collect(back_messages)
    grad_proj = (entity_scale * back_collected).astype(jnp.bfloat16)
    grad_features = lax.dot_general(
        grad_proj, theta, (((1,), (1,)), ((), ())), preferred_element_type=jnp.float32
    ).astype(jnp.bfloat16)
    local_theta = lax.dot_general(
        features, grad_proj, (((0,), (0,)), ((), ())), preferred_element_type=jnp.float32
    )
    grad_theta = lax.psum(local_theta, "ent")
    return (activated, grad_features, grad_theta, grad_weight)


def solution(mesh):
    placed = (
        P("ent", None),
        P(),
        P(("ent", "sec")),
        P(("ent", "sec"), None, None),
        P(("ent", "sec"), None, None),
        P(("ent", "sec"), None),
        P("ent", None),
    )
    return jax.shard_map(
        body,
        mesh=mesh,
        in_specs=placed,
        out_specs=(P("ent", None), P("ent", None), P(), P(("ent", "sec"))),
        check_vma=False,
    )
```

profile of v0, /device:TPU:0, one launch (start us, length us, event | category | flops | bytes accessed | tf_op | source)
XLA Modules:
  0.0 1644.0 jit_solution(5554662827985014451)
XLA Ops:
  9.2 113.5 %scatter_custom_fusion = f32[4096]{0:T(1024)S(1)} fusion(s32[16384]{0:T(1024)S(1)} %bitcast.81, f32[16384]{0:T(1024)S(1)} %bitcast.82, f32[]{:T(128)} %constant.131.clone.1), kind=kCustom, calls=%fused_computation.76 | custom fusion | flops 16384 | bytes 16388 | tf_op jit(solution)/shard_map/scatter-add | solution.py:24
  122.6 68.3 %psum.28 = f32[4096]{0:T(1024)S(1)} all-reduce(f32[4096]{0:T(1024)S(1)} %scatter_custom_fusion), channel_id=1, replica_groups=mesh['ent'=32,'sec'=4] {'ent','sec'}, use_global_device_ids=true, to_apply=%region_1.0 | all-reduce | flops 4096 | bytes 32768 | tf_op jit(solution)/shard_map/psum | solution.py:27
  193.5 113.4 %scatter_custom_fusion.1 = f32[512]{0:T(512)S(1)} fusion(s32[16384]{0:T(1024)S(1)} %bitcast.84, f32[16384]{0:T(1024)S(1)} %bitcast.83, f32[]{:T(128)} %constant.137.clone.1), kind=kCustom, calls=%fused_computation.78 | custom fusion | flops 16384 | bytes 2052 | tf_op jit(solution)/shard_map/scatter-add | solution.py:30
  307.7 79.9 %while.50 = (s32[]{:T(128)}, f32[512,256]{1,0:T(8,128)S(1)}, s32[32,512]{1,0:T(8,128)}, pred[32,512]{1,0:T(8,128)(4,1)S(1)}, s32[32,512]{1,0:T(8,128)}, /*index=...) while((s32[]{:T(128)}, f32[512,256]{1,0:T(8,128)S(1)}, ...), condition=%wide.region_4.5_spmd.clone, body=%wide.region_3.4_spmd.clone.sunk | while | flops 168820736 | bytes 1128617 | solution.py:55
  313.4 1.7 convolution_add_fusion.4
  315.9 1.7 convolution_add_fusion.4
  330.9 1.7 convolution_add_fusion.4
  333.4 1.7 convolution_add_fusion.4
  348.4 1.7 convolution_add_fusion.4
  383.4 1.7 convolution_add_fusion.4
  387.7 2.4 broadcast.21.clone
  390.2 144.5 %while.48 = (s32[]{:T(128)}, f32[32,128,256]{2,1,0:T(8,128)}, s32[32]{0:T(128)S(1)}, s32[32,512]{1,0:T(8,128)}, pred[32,512]{1,0:T(8,128)(4,1)S(1)}, /*index=5*/...) while((s32[]{:T(128)}, f32[32,128,256]{2,1,0:T(8,128)}, ...), condition=%wide.region_6.7_spmd, body=%wide.region_5.6_spmd.sunk | while | flops 168558592 | bytes 408219 | solution.py:73
  534.8 188.6 %reduce-scatter.3.cloned.1.call-done = f32[128,256]{1,0:T(8,128)} async-done(((f32[4096,256]{1,0:T(8,128)}), f32[128,256]{1,0:T(8,128)}) %reduce-scatter.3.cloned.1.call-update) | async-done | bytes 131088 | tf_op jit(solution)/shard_map/reduce_scatter | solution.py:77
  723.4 32.8 %all-reduce.4.cloned.1.call-done = f32[128,256]{1,0:T(8,128)} async-done(((f32[128,256]{1,0:T(8,128)}), f32[128,256]{1,0:T(8,128)}) %all-reduce.4.cloned.1.call-update) | async-done | bytes 131088 | tf_op jit(solution)/shard_map/psum | solution.py:80
  758.0 73.9 %all-gather.5.cloned.1.call-done = bf16[4096,256]{1,0:T(8,128)(2,1)} async-done(((bf16[128,256]{1,0:T(8,128)(2,1)}), bf16[4096,256]{1,0:T(8,128)(2,1)}) %all-gather.5.cloned.1.call-update) | async-done | bytes 2097168 | tf_op jit(solution)/shard_map/all_gather | solution.py:96
  831.9 79.9 %while.51 = (s32[]{:T(128)}, f32[512,256]{1,0:T(8,128)S(1)}, s32[32,512]{1,0:T(8,128)}, pred[32,512]{1,0:T(8,128)(4,1)S(1)}, s32[32,512]{1,0:T(8,128)}, /*index=...) while((s32[]{:T(128)}, f32[512,256]{1,0:T(8,128)S(1)}, ...), condition=%wide.region_10.11_spmd.clone, body=%wide.region_9.10_spmd.clone.sunk | while | flops 168820736 | bytes 1128617 | solution.py:55
  912.0 2.4 broadcast.21
  914.4 144.5 %while.49 = (s32[]{:T(128)}, f32[32,128,256]{2,1,0:T(8,128)}, s32[32]{0:T(128)S(1)}, s32[32,512]{1,0:T(8,128)}, pred[32,512]{1,0:T(8,128)(4,1)S(1)}, /*index=5*/...) while((s32[]{:T(128)}, f32[32,128,256]{2,1,0:T(8,128)}, ...), condition=%wide.region_12.13_spmd, body=%wide.region_11.12_spmd.sunk | while | flops 168558592 | bytes 408219 | solution.py:73
  1059.0 190.6 %reduce-scatter.5.cloned.1.call-done = f32[128,256]{1,0:T(8,128)} async-done(((f32[4096,256]{1,0:T(8,128)}), f32[128,256]{1,0:T(8,128)}) %reduce-scatter.5.cloned.1.call-update) | async-done | bytes 131088 | tf_op jit(solution)/shard_map/reduce_scatter | solution.py:77
  1249.7 32.8 %all-reduce.6.cloned.1.call-done = f32[128,256]{1,0:T(8,128)} async-done(((f32[128,256]{1,0:T(8,128)}), f32[128,256]{1,0:T(8,128)}) %all-reduce.6.cloned.1.call-update) | async-done | bytes 131088 | tf_op jit(solution)/shard_map/psum | solution.py:80
  1282.5 1.9 convolution_bitcast_fusion
  1285.0 1.7 convolution_convert_fusion.4
  1286.8 348.6 %all-reduce.8.cloned.1.call-done = f32[256,256]{0,1:T(8,128)} async-done(((f32[256,256]{0,1:T(8,128)}), f32[256,256]{0,1:T(8,128)}) %all-reduce.8.cloned.1.call-update) | async-done | bytes 262160 | tf_op jit(solution)/shard_map/psum | solution.py:108
  1635.4 1.8 copy.11
  (482 shorter events, 320.6 us)
Async XLA Ops:
  7.2 183.8 %copy-start = (bf16[256,256]{1,0:T(8,128)(2,1)S(1)}, bf16[256,256]{1,0:T(8,128)(2,1)}, u32[]{:S(2)}) copy-start(bf16[256,256]{1,0:T(8,128)(2,1)} %param.16) | copy-start | bytes 393220
  7.2 300.5 %all-gather.3.cloned.1.call-start = ((), (), s32[]{:S(2)}) async-start(), calls=%async_computation.2 | async-start | bytes 2162688 | tf_op jit(solution)/shard_map/all_gather | solution.py:86
  192.6 530.7 %reduce-scatter.3.cloned.1.call-start = ((), (), s32[]{:S(2)}) async-start(), calls=%async_computation.3 | async-start | bytes 4325376 | tf_op jit(solution)/shard_map/reduce_scatter | solution.py:77
  390.1 366.0 %copy-start.2 = (bf16[128,256]{1,0:T(8,128)(2,1)S(1)}, bf16[128,256]{1,0:T(8,128)(2,1)}, u32[]{:S(2)}) copy-start(bf16[128,256]{1,0:T(8,128)(2,1)} %param.21) | copy-start | bytes 196612
  534.7 221.5 %all-reduce.4.cloned.1.call-start = ((), (), s32[]{:S(2)}) async-start(), calls=%async_computation.4 | async-start | bytes 262144 | tf_op jit(solution)/shard_map/psum | solution.py:80
  723.4 108.5 %all-gather.5.cloned.1.call-start = ((), (), s32[]{:S(2)}) async-start(), calls=%async_computation.5 | async-start | bytes 2162688 | tf_op jit(solution)/shard_map/all_gather | solution.py:96
  757.9 491.7 %reduce-scatter.5.cloned.1.call-start = ((), (), s32[]{:S(2)}) async-start(), calls=%async_computation.6 | async-start | bytes 4325376 | tf_op jit(solution)/shard_map/reduce_scatter | solution.py:77
  914.4 368.1 %copy-start.1 = (bf16[128,256]{1,0:T(8,128)(2,1)S(1)}, bf16[128,256]{1,0:T(8,128)(2,1)}, u32[]{:S(2)}) copy-start(bf16[128,256]{1,0:T(8,128)(2,1)} %param.15) | copy-start | bytes 196612
  1059.0 223.6 %all-reduce.6.cloned.1.call-start = ((), (), s32[]{:S(2)}) async-start(), calls=%async_computation.7 | async-start | bytes 262144 | tf_op jit(solution)/shard_map/psum | solution.py:80
  1249.7 385.8 %all-reduce.8.cloned.1.call-start = ((), (), s32[]{:S(2)}) async-start(), calls=%async_computation.8 | async-start | bytes 524288 | tf_op jit(solution)/shard_map/psum | solution.py:108
Sparse Core Ops, SparseCore 0:
  192.7 66.8 all-gather.2
  534.8 188.4 reduce-scatter.2
  725.8 30.3 all-reduce.3
  760.1 71.6 all-gather.4
  1059.1 190.4 reduce-scatter.4
  1252.1 30.3 all-reduce.5
  1285.6 349.7 all-reduce.7
where the time goes:
time: 1670 us; the launch traced here: 1640 us
  waiting for transfers between devices  867 us (52%)
  other arithmetic  231 us (14%)
  matrix products  191 us (11%)
  local copies, waits for them, and re-layouts  145 us (9%)
  loops' own time  126 us (8%)
  blocking collectives  68.3 us (4%)
    reduce_scatter x2, waiting for transfers between devices, collect(): lax.psum_scatter(entity_terms(messages, jnp.int32(0)), 'ent', scatter_dim...  379 us
    psum x1, waiting for transfers between devices, body(): grad_theta = lax.psum(local_theta, 'ent')  349 us
    another operation x2, loops' own time, entity_terms(): pieces = lax.map(block_term, jnp.arange(block_span, dtype=jnp.int32))  125 us
    scatter-add x1, other arithmetic, body(): jax.ops.segment_sum(usable_float.reshape(-1), entity_index.reshape(-1), n...  113 us
    scatter-add x1, other arithmetic, body(): jax.ops.segment_sum(usable_float.reshape(-1), row_lists.reshape(-1), num_...  113 us
    dot_general x64, matrix products, add_block(): jnp.einsum('ps,pf->sf', row_hot, picked, preferred_element_type=jnp.float32)  108 us
    dot_general x64, matrix products, block_term(): jnp.einsum('pw,pf->wf', col_hot, picked, preferred_element_type=jnp.float32)  77.7 us
    all_gather x1, waiting for transfers between devices, body(): lax.all_gather(back_scaled, 'ent', axis=0, tiled=True)  73.9 us
  transfers between devices with their start and end apart: 7, of which 6 were waited for; matrix products, arithmetic and copies ran while one was open for 7% of the time, Pallas kernels for 0%

commit v1 on v0

--- a/solution.py
+++ b/solution.py
@@ -2,6 +2,11 @@
 import jax.numpy as jnp
 from jax import lax
 from jax.sharding import PartitionSpec as P
+
+
+def all_by_exchange(shard, name, dim):
+    sent = jnp.stack([shard] * lax.axis_size(name))
+    return jnp.concatenate(lax.all_to_all(sent, name, 0, 0), axis=dim)
 
 
 def hot_table(indices, live_slots, offset, table_width):
@@ -92,9 +97,7 @@
     sigmoid_pre = jax.nn.sigmoid(preact)
     grad_pre = cotangent.astype(jnp.float32) * sigmoid_pre * (1.0 + preact * (1.0 - sigmoid_pre))
     back_scaled = (entity_scale * grad_pre).astype(jnp.bfloat16)
-    back_gathered = entity_fold(
-        zero_sections, lax.all_gather(back_scaled, "ent", axis=0, tiled=True), jnp.int32(0)
-    )
+    back_gathered = entity_fold(zero_sections, all_by_exchange(back_scaled, "ent", 0), jnp.int32(0))
     grad_weight = jnp.sum(gathered * back_gathered, axis=1) / (1.0 + sec_count)
     back_messages = (section_scale * back_gathered).astype(jnp.bfloat16)
     back_collected = collect(back_messages)

time: 1670 us -> 1610 us (0.964)
  waiting for transfers between devices: 867 us -> 823 us
  matrix products: 191 us -> 165 us
    all_gather x1 -> x0, waiting for transfers between devices: 73.9 us -> none  [body(): lax.all_gather(back_scaled, 'ent', axis=0, tiled=True)]
    all_to_all x0 -> x1, waiting for transfers between devices: none -> 29 us  [all_by_exchange(): return jnp.concatenate(lax.all_to_all(sent, name, 0, 0), axis=dim)]
    dot_general x64, matrix products: 108 us -> 81.6 us  [add_block(): jnp.einsum('ps,pf->sf', row_hot, picked, preferred_element_type=jnp.float32)]
where the time goes in v1:
time: 1610 us; the launch traced here: 1580 us
  waiting for transfers between devices  823 us (51%)
  other arithmetic  231 us (14%)
  matrix products  165 us (10%)
  local copies, waits for them, and re-layouts  147 us (9%)
  loops' own time  126 us (8%)
  blocking collectives  68.3 us (4%)
    reduce_scatter x2, waiting for transfers between devices, collect(): lax.psum_scatter(entity_terms(messages, jnp.int32(0)), 'ent', scatter_dim...  379 us
    psum x1, waiting for transfers between devices, body(): grad_theta = lax.psum(local_theta, 'ent')  349 us
    another operation x2, loops' own time, entity_terms(): pieces = lax.map(block_term, jnp.arange(block_span, dtype=jnp.int32))  125 us
    scatter-add x1, other arithmetic, body(): jax.ops.segment_sum(usable_float.reshape(-1), entity_index.reshape(-1), n...  113 us
    scatter-add x1, other arithmetic, body(): jax.ops.segment_sum(usable_float.reshape(-1), row_lists.reshape(-1), num_...  113 us
    dot_general x64, matrix products, add_block(): jnp.einsum('ps,pf->sf', row_hot, picked, preferred_element_type=jnp.float32)  81.6 us
    dot_general x64, matrix products, block_term(): jnp.einsum('pw,pf->wf', col_hot, picked, preferred_element_type=jnp.float32)  77.7 us
    psum x1, blocking collectives, body(): entity_degree = lax.psum(local_degree, ('ent', 'sec'))  68.3 us
  transfers between devices with their start and end apart: 7, of which 6 were waited for; matrix products, arithmetic and copies ran while one was open for 7% of the time, Pallas kernels for 0%

profile of v1, /device:TPU:0, one launch (start us, length us, event | category | flops | bytes accessed | tf_op | source)
XLA Modules:
  0.0 1583.2 jit_solution(12497327170666534477)
XLA Ops:
  9.2 113.5 %scatter_custom_fusion = f32[4096]{0:T(1024)S(1)} fusion(s32[16384]{0:T(1024)S(1)} %bitcast.83, f32[16384]{0:T(1024)S(1)} %bitcast.84, f32[]{:T(128)} %constant.131.clone.1), kind=kCustom, calls=%fused_computation.76 | custom fusion | flops 16384 | bytes 16388 | tf_op jit(solution)/shard_map/scatter-add | solution.py:29
  122.6 68.3 %psum.28 = f32[4096]{0:T(1024)S(1)} all-reduce(f32[4096]{0:T(1024)S(1)} %scatter_custom_fusion), channel_id=1, replica_groups=mesh['ent'=32,'sec'=4] {'ent','sec'}, use_global_device_ids=true, to_apply=%region_1.0 | all-reduce | flops 4096 | bytes 32768 | tf_op jit(solution)/shard_map/psum | solution.py:32
  193.5 113.4 %scatter_custom_fusion.1 = f32[512]{0:T(512)S(1)} fusion(s32[16384]{0:T(1024)S(1)} %bitcast.86, f32[16384]{0:T(1024)S(1)} %bitcast.85, f32[]{:T(128)} %constant.137.clone.1), kind=kCustom, calls=%fused_computation.78 | custom fusion | flops 16384 | bytes 2052 | tf_op jit(solution)/shard_map/scatter-add | solution.py:35
  307.7 79.9 %while.50 = (s32[]{:T(128)}, f32[512,256]{1,0:T(8,128)S(1)}, s32[32,512]{1,0:T(8,128)}, pred[32,512]{1,0:T(8,128)(4,1)S(1)}, s32[32,512]{1,0:T(8,128)}, /*index=...) while((s32[]{:T(128)}, f32[512,256]{1,0:T(8,128)S(1)}, ...), condition=%wide.region_4.5_spmd.clone, body=%wide.region_3.4_spmd.clone.sunk | while | flops 168820736 | bytes 1128617 | solution.py:60
  313.4 1.7 convolution_add_fusion.4
  315.9 1.7 convolution_add_fusion.4
  318.4 1.7 convolution_add_fusion.4
  320.9 1.7 convolution_add_fusion.4
  323.4 1.7 convolution_add_fusion.4
  387.7 2.4 broadcast.23.clone
  390.1 144.5 %while.48 = (s32[]{:T(128)}, f32[32,128,256]{2,1,0:T(8,128)}, s32[32]{0:T(128)S(1)}, s32[32,512]{1,0:T(8,128)}, pred[32,512]{1,0:T(8,128)(4,1)S(1)}, /*index=5*/...) while((s32[]{:T(128)}, f32[32,128,256]{2,1,0:T(8,128)}, ...), condition=%wide.region_6.7_spmd, body=%wide.region_5.6_spmd.sunk | while | flops 168558592 | bytes 408219 | solution.py:78
  534.7 188.6 %reduce-scatter.3.cloned.1.call-done = f32[128,256]{1,0:T(8,128)} async-done(((f32[4096,256]{1,0:T(8,128)}), f32[128,256]{1,0:T(8,128)}) %reduce-scatter.3.cloned.1.call-update) | async-done | bytes 131088 | tf_op jit(solution)/shard_map/reduce_scatter | solution.py:82
  723.3 32.8 %all-reduce.4.cloned.1.call-done = f32[128,256]{1,0:T(8,128)} async-done(((f32[128,256]{1,0:T(8,128)}), f32[128,256]{1,0:T(8,128)}) %all-reduce.4.cloned.1.call-update) | async-done | bytes 131088 | tf_op jit(solution)/shard_map/psum | solution.py:85
  759.4 9.4 all-to-all-start
  768.9 29.0 %all-to-all-done = bf16[32,128,256]{2,1,0:T(8,128)(2,1)S(1)} async-done(((bf16[32,128,256]{2,1,0:T(8,128)(2,1)}), bf16[32,128,256]{2,1,0:T(8,128)(2,1)S(1)}, u32[]{:S(2)}, u32[]{:S(2)}) %all-to-all-start) | async-done | bytes 2097184 | tf_op jit(solution)/shard_map/all_to_all | solution.py:9
  797.8 53.0 %while.51 = (s32[]{:T(128)}, f32[512,256]{1,0:T(8,128)S(1)}, s32[32,512]{1,0:T(8,128)}, pred[32,512]{1,0:T(8,128)(4,1)S(1)}, s32[32,512]{1,0:T(8,128)}, /*index=...) while((s32[]{:T(128)}, f32[512,256]{1,0:T(8,128)S(1)}, ...), condition=%wide.region_10.11_spmd.clone, body=%wide.region_9.10_spmd.clone.sunk | while | flops 168820736 | bytes 1128617 | solution.py:60
  851.1 2.4 broadcast.23
  853.5 144.5 %while.49 = (s32[]{:T(128)}, f32[32,128,256]{2,1,0:T(8,128)}, s32[32]{0:T(128)S(1)}, s32[32,512]{1,0:T(8,128)}, pred[32,512]{1,0:T(8,128)(4,1)S(1)}, /*index=5*/...) while((s32[]{:T(128)}, f32[32,128,256]{2,1,0:T(8,128)}, ...), condition=%wide.region_12.13_spmd, body=%wide.region_11.12_spmd.sunk | while | flops 168558592 | bytes 408219 | solution.py:78
  998.1 190.9 %reduce-scatter.5.cloned.1.call-done = f32[128,256]{1,0:T(8,128)} async-done(((f32[4096,256]{1,0:T(8,128)}), f32[128,256]{1,0:T(8,128)}) %reduce-scatter.5.cloned.1.call-update) | async-done | bytes 131088 | tf_op jit(solution)/shard_map/reduce_scatter | solution.py:82
  1189.0 32.7 %all-reduce.6.cloned.1.call-done = f32[128,256]{1,0:T(8,128)} async-done(((f32[128,256]{1,0:T(8,128)}), f32[128,256]{1,0:T(8,128)}) %all-reduce.6.cloned.1.call-update) | async-done | bytes 131088 | tf_op jit(solution)/shard_map/psum | solution.py:85
  1221.8 1.9 convolution_bitcast_fusion
  1224.3 1.7 convolution_convert_fusion.4
  1226.0 348.5 %all-reduce.8.cloned.1.call-done = f32[256,256]{0,1:T(8,128)} async-done(((f32[256,256]{0,1:T(8,128)}), f32[256,256]{0,1:T(8,128)}) %all-reduce.8.cloned.1.call-update) | async-done | bytes 262160 | tf_op jit(solution)/shard_map/psum | solution.py:111
  1574.5 1.8 copy.11
  (482 shorter events, 296.9 us)
Async XLA Ops:
  7.2 183.8 %copy-start = (bf16[256,256]{1,0:T(8,128)(2,1)S(1)}, bf16[256,256]{1,0:T(8,128)(2,1)}, u32[]{:S(2)}) copy-start(bf16[256,256]{1,0:T(8,128)(2,1)} %param.16) | copy-start | bytes 393220
  7.2 300.5 %all-gather.2.cloned.1.call-start = ((), (), s32[]{:S(2)}) async-start(), calls=%async_computation.3 | async-start | bytes 2162688 | tf_op jit(solution)/shard_map/all_gather | solution.py:91
  192.6 530.7 %reduce-scatter.3.cloned.1.call-start = ((), (), s32[]{:S(2)}) async-start(), calls=%async_computation.4 | async-start | bytes 4325376 | tf_op jit(solution)/shard_map/reduce_scatter | solution.py:82
  390.1 366.0 %copy-start.2 = (bf16[128,256]{1,0:T(8,128)(2,1)S(1)}, bf16[128,256]{1,0:T(8,128)(2,1)}, u32[]{:S(2)}) copy-start(bf16[128,256]{1,0:T(8,128)(2,1)} %param.21) | copy-start | bytes 196612
  534.7 221.5 %all-reduce.4.cloned.1.call-start = ((), (), s32[]{:S(2)}) async-start(), calls=%async_computation.5 | async-start | bytes 262144 | tf_op jit(solution)/shard_map/psum | solution.py:85
  759.4 38.4 %all-to-all-start = ((bf16[32,128,256]{2,1,0:T(8,128)(2,1)}), bf16[32,128,256]{2,1,0:T(8,128)(2,1)S(1)}, u32[]{:S(2)}, u32[]{:S(2)}) async-start(bf16[32,128,256]{2,1,0:T(8,128)(2,1)} %stack.2), calls=%async_computation.1 | async-start | bytes 4194304 | tf_op jit(solution)/shard_map/all_to_all | solution.py:9
  768.8 420.2 %reduce-scatter.5.cloned.1.call-start = ((), (), s32[]{:S(2)}) async-start(), calls=%async_computation.6 | async-start | bytes 4325376 | tf_op jit(solution)/shard_map/reduce_scatter | solution.py:82
  853.5 368.2 %copy-start.1 = (bf16[128,256]{1,0:T(8,128)(2,1)S(1)}, bf16[128,256]{1,0:T(8,128)(2,1)}, u32[]{:S(2)}) copy-start(bf16[128,256]{1,0:T(8,128)(2,1)} %param.15) | copy-start | bytes 196612
  998.1 223.7 %all-reduce.6.cloned.1.call-start = ((), (), s32[]{:S(2)}) async-start(), calls=%async_computation.7 | async-start | bytes 262144 | tf_op jit(solution)/shard_map/psum | solution.py:85
  1189.0 385.5 %all-reduce.8.cloned.1.call-start = ((), (), s32[]{:S(2)}) async-start(), calls=%async_computation.8 | async-start | bytes 524288 | tf_op jit(solution)/shard_map/psum | solution.py:111
Sparse Core Ops, SparseCore 0:
  192.7 66.8 all-gather.1
  534.8 188.4 reduce-scatter.2
  725.8 30.3 all-reduce.3
  998.2 190.7 reduce-scatter.4
  1191.4 30.2 all-reduce.5
  1224.7 349.8 all-reduce.7
